TPU v7x, 32 devices: a whole 2x2x4 slice. The times are simulated.
32 devices in a mesh: groups: 2 (over y), ctx: 4 (over z), head: 4 (over x, core).
Axes of the slice: x: 2, y: 2, z: 4, core: 2. Of those that a mesh axis runs over, the one named last changes fastest.
Arguments:
- queries: bfloat16 [64, 2048, 128], P(('groups', 'head'), 'ctx'), parts along dimension 0, may hold values from -48 to 48
- key_rows: bfloat16 [8, 2048, 128], P(('groups', 'head'), 'ctx'), parts along dimension 0, may hold values from -6 to 6
- value_rows: bfloat16 [8, 2048, 128], P(('groups', 'head'), 'ctx'), parts along dimension 0, may hold values from -6 to 6
- out_grad: bfloat16 [64, 2048, 128], P(('groups', 'head'), 'ctx'), parts along dimension 0, may hold values from -6 to 6
- link_mask: int32 [32, 11], P(('groups', 'ctx')), parts along dimension 0, may hold values from 0 to 1, as said below
Outputs:
- output: bfloat16 [64, 2048, 128], P(('groups', 'head'), 'ctx'), parts along dimension 0
- query_grad: bfloat16 [64, 2048, 128], P(('groups', 'head'), 'ctx'), parts along dimension 0
- key_grad: bfloat16 [8, 2048, 128], P(('groups', 'head'), 'ctx'), parts along dimension 0
- value_grad: bfloat16 [8, 2048, 128], P(('groups', 'head'), 'ctx'), parts along dimension 0
There are 2 independent parts, one for each index of `groups`. A program takes and returns all parts, laid end to end along the dimension named above; each array names one. Nothing has to cross between parts.
Inputs may be any that keep to these rules, and one draw needn't show every extreme that they name: `link_mask`: column 0 is 1 in every row.
All inputs are finite; a program needn't handle non-finite values.
Results may differ from a plain program's by a relative error of at most 0.028.
Values may be sent and summed in bfloat16 or wider, within the bound.
No kernel may reach another device: no remote copies, remote signals or barrier semaphores. Data moves between devices by JAX's collectives and lax.ppermute only.
A program may use at most 64 MiB of HBM per device.

v0:
```python
import math

import jax
import jax.numpy as jnp
from jax import lax
from jax.sharding import PartitionSpec as P

BLK = 128
NOFF = 11


def from_behind(value, axis, steps):
    count = lax.axis_size(axis)
    first, last = (max(0, -steps), min(count, count - steps))
    return lax.ppermute(value, axis, [(source, source + steps) for source in range(first, last)])


def slot_table(block_count, ctx_size):
    entries = []
    for slot_id in range(NOFF):
        offset = 0 if slot_id == 0 else 2 ** (slot_id - 1)
        if offset < block_count:
            entries.append((slot_id, offset, 0))
        elif offset // block_count < ctx_size:
            entries.append((slot_id, offset, offset // block_count))
    return entries


def near_piece(local_blocks, prev_blocks, offset, first_block, span_count):
    block_count = local_blocks.shape[0]
    last_block = first_block + span_count
    middle = min(max(offset, first_block), last_block)
    pieces = []
    if middle > first_block:
        pieces.append(
            prev_blocks[first_block - offset + block_count : middle - offset + block_count]
        )
    if last_block > middle:
        pieces.append(local_blocks[middle - offset : last_block - offset])
    if len(pieces) > 1:
        return jnp.concatenate(pieces, axis=0)
    return pieces[0]


def local(queries, key_rows, value_rows, out_grad, link_mask):
    heads_local, row_count, head_size = queries.shape
    block_count = row_count // BLK
    ctx_size = lax.axis_size("ctx")
    device_index = lax.axis_index("ctx")
    inv_root = 1.0 / math.sqrt(head_size)
    key_value = jnp.concatenate([key_rows[0], value_rows[0]], axis=1)
    entries = slot_table(block_count, ctx_size)
    distances = sorted(set((entry[2] for entry in entries if entry[2] > 0)))
    copies = {}
    for distance in distances:
        copies[distance] = from_behind(key_value, "ctx", distance)

    def to_blocks(array):
        return array.reshape(block_count, BLK, 2 * head_size)

    local_blocks = to_blocks(key_value)
    far_blocks = {distance: to_blocks(copies[distance]) for distance in distances}
    prev_blocks = far_blocks[1]
    own_grads = jnp.zeros((block_count, BLK, 2 * head_size), jnp.float32)
    pending = {
        distance: jnp.zeros((block_count, BLK, 2 * head_size), jnp.float32)
        for distance in distances
    }
    causal = jnp.arange(BLK)[None, :] <= jnp.arange(BLK)[:, None]
    group_size = min(block_count, max(1, 512 // (heads_local * BLK)))
    outputs = []
    query_grads = []
    for first_block in range(0, block_count, group_size):
        span_count = min(group_size, block_count - first_block)
        last_block = first_block + span_count
        block_ids = device_index * block_count + jnp.arange(first_block, last_block)
        pieces = []
        allowed = []
        for slot_id, offset, distance in entries:
            if distance == 0:
                pieces.append(
                    near_piece(local_blocks, prev_blocks, offset, first_block, span_count)
                )
            else:
                pieces.append(far_blocks[distance][first_block:last_block])
            link_live = (link_mask[first_block:last_block, slot_id] == 1) & (block_ids >= offset)
            if offset == 0:
                allowed.append(link_live[:, None, None] & causal[None])
            else:
                allowed.append(jnp.broadcast_to(link_live[:, None, None], (span_count, BLK, BLK)))
        gathered = jnp.concatenate(pieces, axis=1)
        key_part = gathered[..., :head_size]
        value_part = gathered[..., head_size:]
        mask_all = jnp.concatenate(allowed, axis=2)
        query_part = queries[:, first_block * BLK : last_block * BLK].reshape(
            heads_local, span_count, BLK, head_size
        )
        grad_part = out_grad[:, first_block * BLK : last_block * BLK].reshape(
            heads_local, span_count, BLK, head_size
        )
        scores = (
            jnp.einsum("hgtd,gkd->hgtk", query_part, key_part, preferred_element_type=jnp.float32)
            * inv_root
        )
        scores = jnp.where(mask_all[None], scores, -jnp.inf)
        row_max = jnp.max(scores, axis=-1, keepdims=True)
        log_total = row_max + jnp.log(jnp.sum(jnp.exp(scores - row_max), axis=-1, keepdims=True))
        weights = jnp.exp(scores - log_total)
        weights_low = weights.astype(jnp.bfloat16)
        output = jnp.einsum(
            "hgtk,gkd->hgtd", weights_low, value_part, preferred_element_type=jnp.float32
        ).astype(jnp.bfloat16)
        row_dot = jnp.sum(
            grad_part.astype(jnp.float32) * output.astype(jnp.float32), axis=-1, keepdims=True
        )
        grad_weights = jnp.einsum(
            "hgtd,gkd->hgtk", grad_part, value_part, preferred_element_type=jnp.float32
        )
        grad_scores = (weights * (grad_weights - row_dot) * inv_root).astype(jnp.bfloat16)
        query_grad = jnp.einsum(
            "hgtk,gkd->hgtd", grad_scores, key_part, preferred_element_type=jnp.float32
        ).astype(jnp.bfloat16)
        key_part_grad = jnp.einsum(
            "hgtk,hgtd->gkd", grad_scores, query_part, preferred_element_type=jnp.float32
        )
        value_part_grad = jnp.einsum(
            "hgtk,hgtd->gkd", weights_low, grad_part, preferred_element_type=jnp.float32
        )
        joined_grads = jnp.concatenate([key_part_grad, value_part_grad], axis=-1)
        joined_grads = joined_grads.reshape(span_count, len(entries), BLK, 2 * head_size)
        for position, (slot_id, offset, distance) in enumerate(entries):
            slot_grad = joined_grads[:, position]
            if distance > 0:
                pending[distance] = pending[distance].at[first_block:last_block].add(slot_grad)
            else:
                middle = min(max(offset, first_block), last_block)
                if middle > first_block:
                    pending[1] = (
                        pending[1]
                        .at[first_block - offset + block_count : middle - offset + block_count]
                        .add(slot_grad[: middle - first_block])
                    )
                if last_block > middle:
                    own_grads = own_grads.at[middle - offset : last_block - offset].add(
                        slot_grad[middle - first_block :]
                    )
        outputs.append(output.reshape(heads_local, span_count * BLK, head_size))
        query_grads.append(query_grad.reshape(heads_local, span_count * BLK, head_size))
    arrived = None
    for distance in reversed(distances):
        running = pending[distance] if arrived is None else pending[distance] + arrived
        arrived = from_behind(running, "ctx", -max(distance // 2, 1))
    own_grads = own_grads + arrived
    summed = own_grads.reshape(row_count, 2 * head_size)
    key_grad = summed[:, :head_size].astype(jnp.bfloat16)[None]
    value_grad = summed[:, head_size:].astype(jnp.bfloat16)[None]
    return (
        jnp.concatenate(outputs, axis=1),
        jnp.concatenate(query_grads, axis=1),
        key_grad,
        value_grad,
    )


def solution(mesh):
    return jax.shard_map(
        local,
        mesh=mesh,
        in_specs=(
            P(("groups", "head"), "ctx", None),
            P(("groups", "head"), "ctx", None),
            P(("groups", "head"), "ctx", None),
            P(("groups", "head"), "ctx", None),
            P(("groups", "ctx"), None),
        ),
        out_specs=(
            P(("groups", "head"), "ctx", None),
            P(("groups", "head"), "ctx", None),
            P(("groups", "head"), "ctx", None),
            P(("groups", "head"), "ctx", None),
        ),
        check_vma=False,
    )
```

profile of v0, /device:TPU:0, one launch (start us, length us, event | category | flops | bytes accessed | tf_op | source)
XLA Modules:
  0.0 84.8 jit_solution(2241499861576197564)
XLA Ops:
  0.6 1.7 %pad_maximum_fusion.2 = bf16[512,256]{1,0:T(8,128)(2,1)} fusion(bf16[512,128]{1,0:T(8,128)(2,1)} %bitcast.589, bf16[512,128]{1,0:T(8,128)(2,1)} %bitcast.593), kind=kLoop, calls=%fused_computation.115 | loop fusion | flops 524288 | bytes 524288 | tf_op jit(solution)/shard_map/concatenate | solution.py:51
  2.3 5.8 %collective-permute-start = (bf16[512,256]{1,0:T(8,128)(2,1)}, bf16[512,256]{1,0:T(8,128)(2,1)}, u32[]{:S(2)}, u32[]{:S(2)}) collective-permute-start(bf16[512,256]{1,0:T(8,128)(2,1)} %pad_maximum_fusion.2), channel_id=1, source_target_pairs={{0,4},{4,8},{8,12},{1,5},{5,9},{9,13},{2,6},{6,10},{10,14},{3,7},{... | collective-permute-start | bytes 786440 | tf_op jit(solution)/shard_map/ppermute | solution.py:15
  8.1 4.5 %collective-permute-start.1 = (bf16[512,256]{1,0:T(8,128)(2,1)}, bf16[512,256]{1,0:T(8,128)(2,1)}, u32[]{:S(2)}, u32[]{:S(2)}) collective-permute-start(bf16[512,256]{1,0:T(8,128)(2,1)} %pad_maximum_fusion.2), channel_id=1, source_target_pairs={{0,8},{4,12},{1,9},{5,13},{2,10},{6,14},{3,11},{7,15},{16,24},{20,... | collective-permute-start | bytes 786440 | tf_op jit(solution)/shard_map/ppermute | solution.py:15
  12.6 1.3 %slice.773 = s32[1,1]{1,0:T(1,128)} slice(s32[4,11]{1,0:T(4,128)} %param.49), slice={[3:4], [3:4]} | slice | bytes 8 | tf_op jit(solution)/shard_map/slice | solution.py:86
  13.9 2.1 %fusion.172 = (s32[1,1]{1,0:T(1,128)}, s32[1,1]{1,0:T(1,128)}, s32[1,1]{1,0:T(1,128)}, s32[1,1]{1,0:T(1,128)}, s32[1,1]{1,0:T(1,128)}, /*index=5*/s32[1,1]{1,0:T...) fusion(s32[4,11]{1,0:T(4,128)} %param.49), kind=kLoop, calls=%fused_computation.291 | loop fusion | bytes 152 | tf_op jit(solution)/shard_map/slice | solution.py:86
  16.0 0.8 constant_dynamic-update-slice_fusion.24
  29.6 1.3 %fusion.171 = (bf16[8,128,128]{2,1,0:T(8,128)(2,1)S(1)}, bf16[8,128,128]{2,1,0:T(8,128)(2,1)S(1)}, bf16[8,128,128]{2,1,0:T(8,128)(2,1)S(1)}, bf16[8,128,128]{2,1,0:T(8,128)(2,1)S(1)}) fusion(bf16[8,512,128]{2,1,0:T(8,128)(2,1)} %param.48), kind=kLoop, calls=%fused_computation.290 | loop fusion | bytes 2097152
  32.6 0.8 constant_dynamic-update-slice_fusion.3
  33.5 0.8 constant_dynamic-update-slice_fusion.2
  34.3 0.9 %constant_dynamic-update-slice_fusion.1 = (bf16[1,640,256]{2,1,0:T(8,128)(2,1)S(1)}, bf16[1,640,256]{2,1,0:T(8,128)(2,1)S(1)}, bf16[1,640,256]{2,1,0:T(8,128)(2,1)S(1)}, bf16[1,640,256]{2,1,0:T(8,128)(2,1)S(1)}) fusion(bf16[1,640,256]{2,1,0:T(8,128)(2,1)S(1)} %constant_dynamic-update-slice_fusion.2, bf16[512,256]{1,0:T(8,128)(2,1)} %collective-permute-done, ...), kind=kLoop, calls=%fused_computation.218 | loop fusion | bytes 458752
  35.2 0.8 constant_dynamic-update-slice_fusion.11
  36.1 1.0 %constant_dynamic-update-slice_fusion = (bf16[1,640,256]{2,1,0:T(8,128)(2,1)S(1)}, bf16[1,640,256]{2,1,0:T(8,128)(2,1)S(1)}, bf16[1,640,256]{2,1,0:T(8,128)(2,1)S(1)}, bf16[1,640,256]{2,1,0:T(8,128)(2,1)S(1)}) fusion(bf16[1,640,256]{2,1,0:T(8,128)(2,1)S(1)} %get-tuple-element.276, bf16[512,256]{1,0:T(8,128)(2,1)} %collective-permute-done.1, ...), kind=kLoop, calls=%fused_computation.217 | loop fusion | bytes 524288 | tf_op jit(solution)/shard_map/concatenate | solution.py:91
  37.1 0.5 fusion.176
  37.6 0.4 exponential_reduce_fusion.3
  38.3 0.4 fusion.67
  38.7 0.4 copy-done
  39.2 0.8 fusion.7
  39.9 0.6 convolution_bitcast_fusion.6
  40.5 0.6 fusion.61
  41.1 0.6 convolution_bitcast_fusion.7
  42.0 0.7 copy-done.7
  42.6 0.5 fusion.173
  43.1 0.4 exponential_reduce_fusion
  43.9 0.4 fusion.64
  44.3 0.8 fusion.1
  45.1 0.6 convolution_bitcast_fusion
  45.6 0.6 fusion.52
  46.3 0.6 convolution_bitcast_fusion.1
  46.9 0.5 fusion.174
  48.1 0.4 fusion.65
  48.6 0.8 fusion.3
  49.3 0.6 convolution_bitcast_fusion.2
  49.9 0.6 convolution_bitcast_fusion.3
  50.5 0.7 fusion.175
  51.2 0.4 exponential_reduce_fusion.2
  51.9 0.4 fusion.66
  52.4 0.7 fusion.5
  53.1 0.6 convolution_bitcast_fusion.4
  53.7 0.6 convolution_bitcast_fusion.5
  54.7 1.3 %collective-permute-start.2 = (f32[4,128,256]{1,2,0:T(8,128)S(1)}, f32[4,128,256]{1,2,0:T(8,128)S(1)}, u32[]{:S(2)}, u32[]{:S(2)}) collective-permute-start(f32[4,128,256]{1,2,0:T(8,128)S(1)} %get-tuple-element.256), channel_id=1, source_target_pairs={{4,0},{8,4},{12,8},{5,1},{9,5},{13,9},{6,2},{10,6},{14,10},{7,3},{... | collective-permute-start | bytes 1572872 | tf_op jit(solution)/shard_map/ppermute | solution.py:15
  56.0 0.6 fusion.55
  56.6 0.6 fusion.58
  57.2 1.0 %pad_maximum_fusion.1 = bf16[8,512,128]{2,1,0:T(8,128)(2,1)} fusion(bf16[8,128,128]{2,1,0:T(8,128)(2,1)S(1)} %fusion.52, bf16[8,128,128]{2,1,0:T(8,128)(2,1)S(1)} %fusion.55, bf16[8,128,128]{2,1,0:T(8,128)(2,1)S(1)} %fusion.58, bf16[8,128,128]{2,1,0:T(8,128)(2,1)S(1)} %fusion.61), kind=kLoop, calls=%fused_computation.69 | loop fusion | flops 4194304 | bytes 2097152 | tf_op jit(solution)/shard_map/concatenate | solution.py:159
  58.3 11.4 %collective-permute-done.2 = f32[4,128,256]{1,2,0:T(8,128)S(1)} collective-permute-done((f32[4,128,256]{1,2,0:T(8,128)S(1)}, f32[4,128,256]{1,2,0:T(8,128)S(1)}, u32[]{:S(2)}, u32[]{:S(2)}) %collective-permute-start.2) | collective-permute-done | bytes 524320 | tf_op jit(solution)/shard_map/ppermute | solution.py:15
  69.7 1.3 %collective-permute-start.3 = (f32[4,128,256]{1,2,0:T(8,128)S(1)}, f32[4,128,256]{1,2,0:T(8,128)S(1)}, u32[]{:S(2)}, u32[]{:S(2)}) collective-permute-start(f32[4,128,256]{1,2,0:T(8,128)S(1)} %add.227), channel_id=1, source_target_pairs={{4,0},{8,4},{12,8},{5,1},{9,5},{13,9},{6,2},{10,6},{14,10},{7,3},{... | collective-permute-start | bytes 1572872 | tf_op jit(solution)/shard_map/ppermute | solution.py:15
  71.2 1.3 %copy.75 = bf16[8,512,128]{2,1,0:T(8,128)(2,1)} copy(bf16[8,512,128]{1,2,0:T(8,128)(2,1)S(1)} %pad_maximum_fusion) | data formatting | bytes 2097152
  72.6 11.3 %collective-permute-done.3 = f32[4,128,256]{1,2,0:T(8,128)S(1)} collective-permute-done((f32[4,128,256]{1,2,0:T(8,128)S(1)}, f32[4,128,256]{1,2,0:T(8,128)S(1)}, u32[]{:S(2)}, u32[]{:S(2)}) %collective-permute-start.3) | collective-permute-done | bytes 524320 | tf_op jit(solution)/shard_map/ppermute | solution.py:15
  84.1 0.7 slice_bitcast_fusion.24
  (69 shorter events, 4.4 us)
Async XLA Ops:
  2.3 30.2 %copy-start.2 = (bf16[1,512,128]{2,1,0:T(8,128)(2,1)S(1)}, bf16[1,512,128]{2,1,0:T(8,128)(2,1)}, u32[]{:S(2)}) copy-start(bf16[1,512,128]{2,1,0:T(8,128)(2,1)} %param.47) | copy-start | bytes 393220
  2.3 30.2 %copy-start.3 = (bf16[1,512,128]{2,1,0:T(8,128)(2,1)S(1)}, bf16[1,512,128]{2,1,0:T(8,128)(2,1)}, u32[]{:S(2)}) copy-start(bf16[1,512,128]{2,1,0:T(8,128)(2,1)} %param.46) | copy-start | bytes 393220
  2.3 30.3 %collective-permute-start = (bf16[512,256]{1,0:T(8,128)(2,1)}, bf16[512,256]{1,0:T(8,128)(2,1)}, u32[]{:S(2)}, u32[]{:S(2)}) collective-permute-start(bf16[512,256]{1,0:T(8,128)(2,1)} %pad_maximum_fusion.2), channel_id=1, source_target_pairs={{0,4},{4,8},{8,12},{1,5},{5,9},{9,13},{2,6},{6,10},{10,14},{3,7},{... | collective-permute-start | bytes 786440 | tf_op jit(solution)/shard_map/ppermute | solution.py:15
  8.1 28.0 %collective-permute-start.1 = (bf16[512,256]{1,0:T(8,128)(2,1)}, bf16[512,256]{1,0:T(8,128)(2,1)}, u32[]{:S(2)}, u32[]{:S(2)}) collective-permute-start(bf16[512,256]{1,0:T(8,128)(2,1)} %pad_maximum_fusion.2), channel_id=1, source_target_pairs={{0,8},{4,12},{1,9},{5,13},{2,10},{6,14},{3,11},{7,15},{16,24},{20,... | collective-permute-start | bytes 786440 | tf_op jit(solution)/shard_map/ppermute | solution.py:15
  30.9 6.2 %copy-start.1 = (bf16[8,512,128]{2,1,0:T(8,128)(2,1)S(1)}, bf16[8,512,128]{2,1,0:T(8,128)(2,1)}, u32[]{:S(2)}) copy-start(bf16[8,512,128]{2,1,0:T(8,128)(2,1)} %param.45) | copy-start | bytes 3145732
  31.0 0.6 copy-start.6
  31.1 0.6 copy-start.4
  38.0 1.2 %copy-start = (bf16[8,512,128]{2,1,0:T(8,128)(2,1)S(1)}, bf16[8,512,128]{2,1,0:T(8,128)(2,1)}, u32[]{:S(2)}) copy-start(bf16[8,512,128]{2,1,0:T(8,128)(2,1)} %param.48) | copy-start | bytes 3145732
  41.7 0.9 %copy-start.7 = (pred[1,128,640]{1,2,0:T(8,128)(4,1)S(1)}, pred[1,128,640]{1,2,0:T(8,128)(4,1)}, u32[]{:S(2)}) copy-start(pred[1,128,640]{1,2,0:T(8,128)(4,1)} %copy-done.6) | copy-start | bytes 245764
  45.1 1.8 %copy-start.5 = (pred[1,128,640]{1,2,0:T(8,128)(4,1)S(1)}, pred[1,128,640]{1,2,0:T(8,128)(4,1)}, u32[]{:S(2)}) copy-start(pred[1,128,640]{1,2,0:T(8,128)(4,1)} %copy-done.4) | copy-start | bytes 245764
  54.7 15.0 %collective-permute-start.2 = (f32[4,128,256]{1,2,0:T(8,128)S(1)}, f32[4,128,256]{1,2,0:T(8,128)S(1)}, u32[]{:S(2)}, u32[]{:S(2)}) collective-permute-start(f32[4,128,256]{1,2,0:T(8,128)S(1)} %get-tuple-element.256), channel_id=1, source_target_pairs={{4,0},{8,4},{12,8},{5,1},{9,5},{13,9},{6,2},{10,6},{14,10},{7,3},{... | collective-permute-start | bytes 1572872 | tf_op jit(solution)/shard_map/ppermute | solution.py:15
  69.7 14.1 %collective-permute-start.3 = (f32[4,128,256]{1,2,0:T(8,128)S(1)}, f32[4,128,256]{1,2,0:T(8,128)S(1)}, u32[]{:S(2)}, u32[]{:S(2)}) collective-permute-start(f32[4,128,256]{1,2,0:T(8,128)S(1)} %add.227), channel_id=1, source_target_pairs={{4,0},{8,4},{12,8},{5,1},{9,5},{13,9},{6,2},{10,6},{14,10},{7,3},{... | collective-permute-start | bytes 1572872 | tf_op jit(solution)/shard_map/ppermute | solution.py:15
where the time goes:
time: 85.7 us; the launch traced here: 84.8 us
  waiting for transfers between devices  22.7 us (26%)
  matrix products  14 us (16%)
  between operations  14 us (16%)
  local copies, waits for them, and re-layouts  13.9 us (16%)
  starting transfers between devices  12.9 us (15%)
  other arithmetic  7.31 us (9%)
    ppermute x4, waiting for transfers between devices, from_behind(): lax.ppermute(value, axis, [(source, source + steps) for source in range(f...  22.7 us
    ppermute x4, starting transfers between devices, from_behind(): lax.ppermute(value, axis, [(source, source + steps) for source in range(f...  12.9 us
    unnamed x38, local copies, waits for them, and re-layouts  8.52 us
    slice x2, local copies, waits for them, and re-layouts, local(): link_mask[first_block:last_block, slot_id] == 1  3.35 us
    dot_general x4, matrix products, local(): jnp.einsum('hgtd,gkd->hgtk', grad_part, value_part, preferred_element_typ...  3.01 us
    dot_general x4, matrix products, local(): jnp.einsum('hgtk,gkd->hgtd', grad_scores, key_part, preferred_element_typ...  2.47 us
    dot_general x4, matrix products, local(): jnp.einsum('hgtk,hgtd->gkd', grad_scores, query_part, preferred_element_t...  2.3 us
    dot_general x4, matrix products, local(): jnp.einsum('hgtk,hgtd->gkd', weights_low, grad_part, preferred_element_ty...  2.27 us
  transfers between devices with their start and end apart: 4, of which 2 were waited for; matrix products, arithmetic and copies ran while one was open for 16% of the time, Pallas kernels for 0%

commit v1 on v0

v1 whole, which is shorter than its diff:
```python
import functools
import math

import jax
import jax.numpy as jnp
from jax import lax
from jax.experimental import pallas as pl
from jax.experimental.pallas import tpu as pltpu
from jax.sharding import PartitionSpec as P

BLK = 128
NOFF = 11
NEG = -1e30
LOG2E = 1.4426950408889634
F32 = jnp.float32
BF16 = jnp.bfloat16


def shift(value, axis, steps):
    count = lax.axis_size(axis)
    first, last = (max(0, -steps), min(count, count - steps))
    return lax.ppermute(value, axis, [(source, source + steps) for source in range(first, last)])


def slot_table(block_count, ctx_size):
    entries = []
    for slot_id in range(NOFF):
        offset = 0 if slot_id == 0 else 2 ** (slot_id - 1)
        if offset < block_count:
            entries.append((slot_id, offset, 0))
        elif offset // block_count < ctx_size:
            entries.append((slot_id, offset, offset // block_count))
    return entries


def dot_nt(a, b):
    return lax.dot_general(a, b, (((1,), (1,)), ((), ())), preferred_element_type=F32)


def dot_nn(a, b):
    return lax.dot_general(a, b, (((1,), (0,)), ((), ())), preferred_element_type=F32)


def causal(width):
    key = lax.broadcasted_iota(jnp.int32, (BLK, width), 0)
    row = lax.broadcasted_iota(jnp.int32, (BLK, width), 1)
    return key <= lax.rem(row, BLK)


def bias_of(live_ref, step, entry):
    return jnp.where(live_ref[step, entry] == 1, 0.0, NEG).astype(F32)


def near_start(step, offset, block_count):
    return pl.multiple_of((step + block_count - offset) * BLK, BLK)


def near_forward(near, pairs, live_ref, q_ref, k_ref, v_ref, kp_ref, vp_ref, stat_ref, acc_ref, kcat, vtcat):
    step = pl.program_id(0)
    rows = k_ref.shape[0]
    blocks = rows // BLK
    size = k_ref.shape[1]
    scale = LOG2E / math.sqrt(size)

    @pl.when(step == 0)
    def _():
        kcat[:rows] = kp_ref[...]
        kcat[rows:] = k_ref[...]
        vtcat[:, :rows] = vp_ref[...].T
        vtcat[:, rows:] = v_ref[...].T

    starts = [near_start(step, offset, blocks) for _, (_, offset, _) in near]
    keys = jnp.concatenate([kcat[pl.ds(start, BLK), :] for start in starts], axis=0)
    values_t = jnp.concatenate([vtcat[:, pl.ds(start, BLK)] for start in starts], axis=1)
    biases = [bias_of(live_ref, step, entry) for entry, _ in near]
    heads = q_ref.shape[0]
    wide = pairs * BLK
    mask = causal(wide)
    for first in range(0, heads, pairs):
        lanes = slice(first * BLK, first * BLK + wide)
        q = q_ref[first : first + pairs].reshape(wide, size)
        scores = dot_nt(keys, q) * scale
        parts = [scores[n * BLK : (n + 1) * BLK] for n in range(len(near))]
        parts[0] = jnp.where(mask, parts[0], NEG)
        top = None
        for part, bias in zip(parts, biases):
            part_top = jnp.max(part, axis=0, keepdims=True) + bias
            top = part_top if top is None else jnp.maximum(top, part_top)
        exps = [jnp.exp2(part - (top - bias)) for part, bias in zip(parts, biases)]
        total = sum(jnp.sum(part, axis=0, keepdims=True) for part in exps)
        low = jnp.concatenate([part.astype(BF16) for part in exps], axis=0)
        stat_ref[0, 0:1, lanes] = top
        stat_ref[0, 1:2, lanes] = total
        acc_ref[0, :, lanes] = dot_nn(values_t, low)


def far_both(far, pairs, live_ref, q_ref, do_ref, kf_ref, vf_ref, stat_ref, acc_ref, o_ref, dkf_ref, dvf_ref, ds_ref, fin_ref):
    step = pl.program_id(0)
    count = len(far)
    heads, _, size = q_ref.shape
    inv_root = 1.0 / math.sqrt(size)
    scale = LOG2E * inv_root
    keys = kf_ref[...].reshape(count * BLK, size)
    values = vf_ref[...].reshape(count * BLK, size)
    values_t = values.T
    biases = [bias_of(live_ref, step, entry) for entry, _ in far]
    wide = pairs * BLK
    dk = jnp.zeros((count * BLK, size), F32)
    dv = jnp.zeros((count * BLK, size), F32)
    for first in range(0, heads, pairs):
        lanes = slice(first * BLK, first * BLK + wide)
        q = q_ref[first : first + pairs].reshape(wide, size)
        do = do_ref[first : first + pairs].reshape(wide, size)
        scores = dot_nt(keys, q) * scale
        grad_w = dot_nt(values, do)
        parts = [scores[n * BLK : (n + 1) * BLK] for n in range(count)]
        near_top = stat_ref[0, 0:1, lanes]
        top = near_top
        for part, bias in zip(parts, biases):
            top = jnp.maximum(top, jnp.max(part, axis=0, keepdims=True) + bias)
        exps = [jnp.exp2(part - (top - bias)) for part, bias in zip(parts, biases)]
        fade = jnp.exp2(near_top - top)
        total = stat_ref[0, 1:2, lanes] * fade
        total = total + sum(jnp.sum(part, axis=0, keepdims=True) for part in exps)
        inverse = 1.0 / total
        weights = jnp.concatenate(exps, axis=0) * inverse
        low = weights.astype(BF16)
        out_t = acc_ref[0, :, lanes] * (fade * inverse) + dot_nn(values_t, low)
        out_low_t = out_t.astype(BF16)
        o_ref[first : first + pairs] = out_low_t.T.reshape(pairs, BLK, size)
        row_dot = jnp.sum(out_low_t.astype(F32) * do.T.astype(F32), axis=0, keepdims=True)
        ds = (weights * (grad_w - row_dot)).astype(BF16)
        ds_ref[0, :, lanes] = ds
        fin_ref[0, 0:1, lanes] = top + jnp.log2(total)
        fin_ref[0, 1:2, lanes] = row_dot
        dk += dot_nn(ds, q)
        dv += dot_nn(low, do)
    dkf_ref[...] = (dk * inv_root).astype(BF16).reshape(dkf_ref.shape)
    dvf_ref[...] = dv.astype(BF16).reshape(dvf_ref.shape)


def near_backward(
    near, pairs, live_ref, q_ref, do_ref, k_ref, v_ref, kp_ref, vp_ref, kf_ref, fin_ref, ds_ref,
    dq_ref, dk_ref, dv_ref, dkp_ref, dvp_ref, kcat, vcat, dkcat, dvcat
):
    step = pl.program_id(0)
    rows = k_ref.shape[0]
    blocks = rows // BLK
    heads, _, size = q_ref.shape
    inv_root = 1.0 / math.sqrt(size)
    scale = LOG2E * inv_root

    @pl.when(step == 0)
    def _():
        kcat[:rows] = kp_ref[...]
        kcat[rows:] = k_ref[...]
        vcat[:rows] = vp_ref[...]
        vcat[rows:] = v_ref[...]
        dkcat[...] = jnp.zeros_like(dkcat)
        dvcat[...] = jnp.zeros_like(dvcat)

    starts = [near_start(step, offset, blocks) for _, (_, offset, _) in near]
    keys = jnp.concatenate([kcat[pl.ds(start, BLK), :] for start in starts], axis=0)
    values = jnp.concatenate([vcat[pl.ds(start, BLK), :] for start in starts], axis=0)
    far_count = kf_ref.shape[0]
    all_keys_t = jnp.concatenate([keys, kf_ref[...].reshape(far_count * BLK, size)], axis=0).T
    biases = [bias_of(live_ref, step, entry) for entry, _ in near]
    wide = pairs * BLK
    mask = causal(wide)
    dk = jnp.zeros((len(near) * BLK, size), F32)
    dv = jnp.zeros((len(near) * BLK, size), F32)
    for first in range(0, heads, pairs):
        lanes = slice(first * BLK, first * BLK + wide)
        q = q_ref[first : first + pairs].reshape(wide, size)
        do = do_ref[first : first + pairs].reshape(wide, size)
        scores = dot_nt(keys, q) * scale
        grad_w = dot_nt(values, do)
        log_total = fin_ref[0, 0:1, lanes]
        row_dot = fin_ref[0, 1:2, lanes]
        parts = [scores[n * BLK : (n + 1) * BLK] for n in range(len(near))]
        parts[0] = jnp.where(mask, parts[0], NEG)
        weights = jnp.concatenate(
            [jnp.exp2(part - (log_total - bias)) for part, bias in zip(parts, biases)], axis=0
        )
        ds = (weights * (grad_w - row_dot)).astype(BF16)
        low = weights.astype(BF16)
        dk += dot_nn(ds, q)
        dv += dot_nn(low, do)
        all_ds = jnp.concatenate([ds, ds_ref[0, :, lanes]], axis=0)
        dq_t = (dot_nn(all_keys_t, all_ds) * inv_root).astype(BF16)
        dq_ref[first : first + pairs] = dq_t.T.reshape(pairs, BLK, size)
    for n, start in enumerate(starts):
        dkcat[pl.ds(start, BLK), :] += dk[n * BLK : (n + 1) * BLK]
        dvcat[pl.ds(start, BLK), :] += dv[n * BLK : (n + 1) * BLK]

    @pl.when(step == blocks - 1)
    def _():
        dkp_ref[...] = dkcat[:rows] * inv_root
        dk_ref[...] = dkcat[rows:] * inv_root
        dvp_ref[...] = dvcat[:rows]
        dv_ref[...] = dvcat[rows:]


def local(queries, key_rows, value_rows, out_grad, link_mask):
    heads, rows, size = queries.shape
    blocks = rows // BLK
    ctx_size = lax.axis_size("ctx")
    entries = slot_table(blocks, ctx_size)
    near = [(n, e) for n, e in enumerate(entries) if e[1] <= blocks]
    far = [(n, e) for n, e in enumerate(entries) if e[1] > blocks]
    hops = [e[2] for _, e in far]
    pairs = 2

    keys, values = key_rows[0], value_rows[0]
    with jax.named_scope("hop_k1"):
        k_prev = shift(keys, "ctx", 1)
    with jax.named_scope("hop_v1"):
        v_prev = shift(values, "ctx", 1)
    k_far, v_far = [], []
    k_last, v_last, at = k_prev, v_prev, 1
    for hop in hops:
        with jax.named_scope(f"hop_k{hop}"):
            k_last = shift(k_last, "ctx", hop - at)
        with jax.named_scope(f"hop_v{hop}"):
            v_last = shift(v_last, "ctx", hop - at)
        at = hop
        k_far.append(k_last)
        v_far.append(v_last)
    if len(far) == 1:
        k_far, v_far = k_far[0][None], v_far[0][None]
    else:
        k_far, v_far = jnp.stack(k_far), jnp.stack(v_far)

    block_ids = lax.axis_index("ctx") * blocks + jnp.arange(blocks)
    slot_ids = jnp.array([e[0] for e in entries])
    offsets = jnp.array([e[1] for e in entries])
    live = (link_mask[:, slot_ids] == 1) & (block_ids[:, None] >= offsets[None, :])
    live = live.astype(jnp.int32)

    smem = pl.BlockSpec(memory_space=pltpu.SMEM)
    head_spec = pl.BlockSpec((heads, BLK, size), lambda i: (0, i, 0))
    whole = pl.BlockSpec((rows, size), lambda i: (0, 0))
    far_spec = pl.BlockSpec((len(far), BLK, size), lambda i: (0, i, 0))
    lanes = heads * BLK
    stat_spec = pl.BlockSpec((1, 8, lanes), lambda i: (i, 0, 0))
    acc_spec = pl.BlockSpec((1, size, lanes), lambda i: (i, 0, 0))
    ds_spec = pl.BlockSpec((1, len(far) * BLK, lanes), lambda i: (i, 0, 0))
    stat_shape = jax.ShapeDtypeStruct((blocks, 8, lanes), F32)
    acc_shape = jax.ShapeDtypeStruct((blocks, size, lanes), F32)
    ds_shape = jax.ShapeDtypeStruct((blocks, len(far) * BLK, lanes), BF16)
    far_shape = jax.ShapeDtypeStruct((len(far), rows, size), BF16)
    head_shape = jax.ShapeDtypeStruct(queries.shape, BF16)
    sum_shape = jax.ShapeDtypeStruct((rows, size), F32)

    def cost(slots, matmuls):
        return pl.CostEstimate(
            flops=2 * matmuls * slots * BLK * blocks * lanes * size,
            bytes_accessed=4 * queries.size,
            transcendentals=slots * BLK * blocks * lanes,
        )

    params = pltpu.CompilerParams(dimension_semantics=("arbitrary",), vmem_limit_bytes=40 << 20)
    with jax.named_scope("near_forward"):
        stats, acc = pl.pallas_call(
            functools.partial(near_forward, near, pairs),
            grid=(blocks,),
            in_specs=[smem, head_spec, whole, whole, whole, whole],
            out_specs=[stat_spec, acc_spec],
            out_shape=[stat_shape, acc_shape],
            scratch_shapes=[pltpu.VMEM((2 * rows, size), BF16), pltpu.VMEM((size, 2 * rows), BF16)],
            compiler_params=params,
            cost_estimate=cost(len(near), 2),
            name="near_forward",
        )(live, queries, keys, values, k_prev, v_prev)
    with jax.named_scope("far_both"):
        output, dk_far, dv_far, ds_far, fin = pl.pallas_call(
            functools.partial(far_both, far, pairs),
            grid=(blocks,),
            in_specs=[smem, head_spec, head_spec, far_spec, far_spec, stat_spec, acc_spec],
            out_specs=[head_spec, far_spec, far_spec, ds_spec, stat_spec],
            out_shape=[head_shape, far_shape, far_shape, ds_shape, stat_shape],
            compiler_params=params,
            cost_estimate=cost(len(far), 5),
            name="far_both",
        )(live, queries, out_grad, k_far, v_far, stats, acc)
    with jax.named_scope("near_backward"):
        query_grad, dk_own, dv_own, dk_prev, dv_prev = pl.pallas_call(
            functools.partial(near_backward, near, pairs),
            grid=(blocks,),
            in_specs=[smem, head_spec, head_spec, whole, whole, whole, whole, far_spec, stat_spec, ds_spec],
            out_specs=[head_spec, whole, whole, whole, whole],
            out_shape=[head_shape, sum_shape, sum_shape, sum_shape, sum_shape],
            scratch_shapes=[
                pltpu.VMEM((2 * rows, size), BF16),
                pltpu.VMEM((2 * rows, size), BF16),
                pltpu.VMEM((2 * rows, size), F32),
                pltpu.VMEM((2 * rows, size), F32),
            ],
            compiler_params=params,
            cost_estimate=cost(len(near), 5),
            name="near_backward",
        )(live, queries, out_grad, keys, values, k_prev, v_prev, k_far, fin, ds_far)

    def send_back(pending, prev, own, name):
        arrived = None
        levels = [(hop, pending[n].astype(F32)) for n, hop in enumerate(hops)]
        levels = [(1, prev)] + levels
        for n in reversed(range(len(levels))):
            hop, mine = levels[n]
            below = levels[n - 1][0] if n > 0 else 0
            running = mine if arrived is None else mine + arrived.astype(F32)
            with jax.named_scope(f"back_{name}{hop}"):
                arrived = shift(running.astype(BF16), "ctx", below - hop)
        return (own + arrived.astype(F32)).astype(BF16)[None]

    value_grad = send_back(dv_far, dv_prev, dv_own, "v")
    key_grad = send_back(dk_far, dk_prev, dk_own, "k")
    return output, query_grad, key_grad, value_grad


def solution(mesh):
    split = P(("groups", "head"), "ctx", None)
    return jax.shard_map(
        local,
        mesh=mesh,
        in_specs=(split, split, split, split, P(("groups", "ctx"), None)),
        out_specs=(split, split, split, split),
        check_vma=False,
    )
```

time: 85.7 us -> 58.9 us (0.69)
  Pallas kernels: 0 us -> 24.4 us
  waiting for transfers between devices: 22.7 us -> 7.14 us
  matrix products: 14 us -> 0 us
  between operations: 14 us -> 0.79 us
  local copies, waits for them, and re-layouts: 13.9 us -> 4.47 us
  starting transfers between devices: 12.9 us -> 19.5 us
  other arithmetic: 7.31 us -> 2.17 us
    pallas_call x0 -> x3, Pallas kernels: none -> 24.4 us  [the longest x1 8.84 us: local(): pl.pallas_call(functools.partial(near_backward, near, pairs), grid=(block...]
    ppermute x4 -> x8, waiting for transfers between devices: 22.7 us -> 7.14 us  [shift(): lax.ppermute(value, axis, [(source, source + steps) for source in range(f...]
    dot_general x24 -> x0, matrix products: 14 us -> none  [the longest x4 3.01 us: local(): jnp.einsum('hgtd,gkd->hgtk', grad_part, value_part, preferred_element_typ...]
    ppermute x4 -> x8, starting transfers between devices: 12.9 us -> 19.5 us  [shift(): lax.ppermute(value, axis, [(source, source + steps) for source in range(f...]
    unnamed x38 -> x10, local copies, waits for them, and re-layouts: 8.52 us -> 3.92 us
    slice x2 -> x0, local copies, waits for them, and re-layouts: 3.35 us -> none  [local(): link_mask[first_block:last_block, slot_id] == 1]
    concatenate x3 -> x0, other arithmetic: 2.88 us -> none  [the longest x1 1.7 us: local(): key_value = jnp.concatenate([key_rows[0], value_rows[0]], axis=1)]
    reduce_sum x4 -> x0, other arithmetic: 1.44 us -> none  [local(): jnp.sum(jnp.exp(scores - row_max), axis=-1, keepdims=True)]
  transfers between devices with their start and end apart: 4 -> 8, of which waited for: 2 -> 2; matrix products, arithmetic and copies ran while one was open for 16% -> 5% of each run, Pallas kernels for 0% -> 29%
where the time goes in v1:
time: 58.9 us; the launch traced here: 58.5 us
  Pallas kernels  24.4 us (41%)
  starting transfers between devices  19.5 us (33%)
  waiting for transfers between devices  7.14 us (12%)
  local copies, waits for them, and re-layouts  4.47 us (8%)
  other arithmetic  2.17 us (4%)
  between operations  0.79 us (1%)
    ppermute x8, starting transfers between devices, shift(): lax.ppermute(value, axis, [(source, source + steps) for source in range(f...  19.5 us
    pallas_call x1, Pallas kernels, local(): pl.pallas_call(functools.partial(near_backward, near, pairs), grid=(block...  8.84 us
    pallas_call x1, Pallas kernels, local(): pl.pallas_call(functools.partial(near_forward, near, pairs), grid=(blocks...  7.84 us
    pallas_call x1, Pallas kernels, local(): pl.pallas_call(functools.partial(far_both, far, pairs), grid=(blocks,), i...  7.7 us
    ppermute x8, waiting for transfers between devices, shift(): lax.ppermute(value, axis, [(source, source + steps) for source in range(f...  7.14 us
    unnamed x10, local copies, waits for them, and re-layouts  3.92 us
    broadcast_in_dim x2, other arithmetic, send_back(): return (own + arrived.astype(F32)).astype(BF16)[None]  1.37 us
  transfers between devices with their start and end apart: 8, of which 2 were waited for; matrix products, arithmetic and copies ran while one was open for 5% of the time, Pallas kernels for 29%

profile of v1, /device:TPU:0, one launch (start us, length us, event | category | flops | bytes accessed | tf_op | source)
XLA Modules:
  0.0 58.5 jit_solution(5452314936946804864)
XLA Ops:
  0.6 5.0 %collective-permute-start = (bf16[512,128]{1,0:T(8,128)(2,1)}, bf16[512,128]{1,0:T(8,128)(2,1)S(1)}, u32[]{:S(2)}, u32[]{:S(2)}) collective-permute-start(bf16[512,128]{1,0:T(8,128)(2,1)} %bitcast.17), channel_id=1, source_target_pairs={{0,4},{4,8},{8,12},{1,5},{5,9},{9,13},{2,6},{6,10},{10,14},{3,7},{... | collective-permute-start | bytes 393224 | tf_op jit(solution)/shard_map/hop_k1/ppermute | solution.py:22
  5.6 3.5 %collective-permute-start.2 = (bf16[512,128]{1,0:T(8,128)(2,1)}, bf16[512,128]{1,0:T(8,128)(2,1)S(1)}, u32[]{:S(2)}, u32[]{:S(2)}) collective-permute-start(bf16[512,128]{1,0:T(8,128)(2,1)} %bitcast.20), channel_id=1, source_target_pairs={{0,4},{4,8},{8,12},{1,5},{5,9},{9,13},{2,6},{6,10},{10,14},{3,7},{... | collective-permute-start | bytes 393224 | tf_op jit(solution)/shard_map/hop_v1/ppermute | solution.py:22
  9.1 0.8 %copy.11 = s32[4,11]{0,1:T(8,128)S(1)} copy(s32[4,11]{1,0:T(4,128)} %param.11) | data formatting | bytes 352 | tf_op args[4]
  9.9 0.6 gather_fusion
  10.5 0.1 copy.13
  10.6 0.0 collective-permute-done.kp_ref
  10.6 3.5 %collective-permute-start.1 = (bf16[512,128]{1,0:T(8,128)(2,1)S(1)}, bf16[512,128]{1,0:T(8,128)(2,1)S(1)}, u32[]{:S(2)}, u32[]{:S(2)}) collective-permute-start(bf16[512,128]{1,0:T(8,128)(2,1)S(1)} %collective-permute-done.kp_ref), channel_id=1, source_target_pairs={{0,4},{4,8},{8,12},{1,5},{5,9},{9,13},{2,6},{6,10},{10,14},{3,7},{... | collective-permute-start | bytes 393224 | tf_op jit(solution)/shard_map/hop_k2/ppermute | solution.py:22
  14.1 0.0 collective-permute-done.2.vp_ref
  14.1 2.4 %collective-permute-start.3 = (bf16[512,128]{1,0:T(8,128)(2,1)S(1)}, bf16[512,128]{1,0:T(8,128)(2,1)S(1)}, u32[]{:S(2)}, u32[]{:S(2)}) collective-permute-start(bf16[512,128]{1,0:T(8,128)(2,1)S(1)} %collective-permute-done.2.vp_ref), channel_id=1, source_target_pairs={{0,4},{4,8},{8,12},{1,5},{5,9},{9,13},{2,6},{6,10},{10,14},{3,7},{... | collective-permute-start | bytes 393224 | tf_op jit(solution)/shard_map/hop_v2/ppermute | solution.py:22
  16.5 0.7 %fusion.2.live_ref = s32[4,5]{1,0:T(4,128)S(1)} fusion(pred[5,4]{0,1:T(4,128)(4,1)S(1)} %copy.13, s32[5]{0:T(128)} %constant.17.clone, s32[4]{0:T(128)S(1)} %iota_add_fusion), kind=kLoop, calls=%fused_computation.10 | loop fusion | flops 60 | bytes 136 | tf_op jit(solution)/shard_map/convert_element_type | solution.py:238
  17.2 0.0 copy-start
  17.2 1.2 %copy-done = bf16[8,512,128]{2,1,0:T(8,128)(2,1)S(1)} copy-done((bf16[8,512,128]{2,1,0:T(8,128)(2,1)S(1)}, bf16[8,512,128]{2,1,0:T(8,128)(2,1)}, u32[]{:S(2)}) %copy-start) | copy-done | bytes 1048600
  18.5 0.0 copy-start.2
  18.5 0.9 %copy-done.2 = bf16[1,512,128]{2,1,0:T(8,128)(2,1)S(1)} copy-done((bf16[1,512,128]{2,1,0:T(8,128)(2,1)S(1)}, bf16[1,512,128]{2,1,0:T(8,128)(2,1)}, u32[]{:S(2)}) %copy-start.2) | copy-done | bytes 131096
  19.4 0.0 copy-start.3
  19.4 0.9 %copy-done.3 = bf16[1,512,128]{2,1,0:T(8,128)(2,1)S(1)} copy-done((bf16[1,512,128]{2,1,0:T(8,128)(2,1)S(1)}, bf16[1,512,128]{2,1,0:T(8,128)(2,1)}, u32[]{:S(2)}) %copy-start.3) | copy-done | bytes 131096
  20.3 0.0 copy-start.1
  20.3 7.8 %near_forward.1 = (f32[4,8,1024]{2,1,0:T(8,128)S(1)}, f32[4,128,1024]{2,1,0:T(8,128)S(1)}) custom-call(s32[4,5]{1,0:T(4,128)S(1)} %fusion.2.live_ref, bf16[8,512,128]{2,1,0:T(8,128)(2,1)S(1)} %copy-done, bf16[512,128]{1,0:T(8,128)(2,1)S(1)} %bitcast.18, bf16[512,128]{1,0:T(8,128)(2,1)S(1)} %bitcast.21, bf16[512,128]{1,0:T(8,128)(2,1)S(1)} %collective-permute-done.kp_ref, ...), custom_call_target="tpu_custom_call" | custom-call | flops 1073741824 | bytes 2097152 | tf_op jit(solution)/shard_map/near_forward/near_forward/pallas_call | solution.py:264
  28.1 0.0 collective-permute-done.1
  28.1 0.0 collective-permute-done.3
  28.1 0.0 copy-done.1
  28.2 7.7 %far_both.1 = (bf16[8,512,128]{2,1,0:T(8,128)(2,1)}, bf16[1,512,128]{2,1,0:T(8,128)(2,1)S(1)}, bf16[1,512,128]{2,1,0:T(8,128)(2,1)S(1)}, bf16[4,128,1024]{2,1,0:T(8,128)(2,1)S(1)}, f32[4,8,1024]{2,1,0:T(8,128)S(1)}) custom-call(s32[4,5]{1,0:T(4,128)S(1)} %fusion.2.live_ref, bf16[8,512,128]{2,1,0:T(8,128)(2,1)S(1)} %copy-done, ...), custom_call_target="tpu_custom_call" | custom-call | flops 671088640 | bytes 2097152 | tf_op jit(solution)/shard_map/far_both/far_both/pallas_call | solution.py:276
  35.9 1.3 %collective-permute-start.4 = (bf16[512,128]{1,0:T(8,128)(2,1)S(1)}, bf16[512,128]{1,0:T(8,128)(2,1)S(1)}, u32[]{:S(2)}, u32[]{:S(2)}) collective-permute-start(bf16[512,128]{1,0:T(8,128)(2,1)S(1)} %bitcast.24), channel_id=1, source_target_pairs={{4,0},{8,4},{12,8},{5,1},{9,5},{13,9},{6,2},{10,6},{14,10},{7,3},{... | collective-permute-start | bytes 393224 | tf_op jit(solution)/shard_map/back_k2/ppermute | solution.py:22
  37.1 1.3 %collective-permute-start.6 = (bf16[512,128]{1,0:T(8,128)(2,1)S(1)}, bf16[512,128]{1,0:T(8,128)(2,1)S(1)}, u32[]{:S(2)}, u32[]{:S(2)}) collective-permute-start(bf16[512,128]{1,0:T(8,128)(2,1)S(1)} %bitcast.23), channel_id=1, source_target_pairs={{4,0},{8,4},{12,8},{5,1},{9,5},{13,9},{6,2},{10,6},{14,10},{7,3},{... | collective-permute-start | bytes 393224 | tf_op jit(solution)/shard_map/back_v2/ppermute | solution.py:22
  38.4 8.8 %near_backward.1 = (bf16[8,512,128]{2,1,0:T(8,128)(2,1)}, f32[512,128]{1,0:T(8,128)S(1)}, f32[512,128]{1,0:T(8,128)S(1)}, f32[512,128]{1,0:T(8,128)S(1)}, f32[512,128]{1,0:T(8,128)S(1)}) custom-call(s32[4,5]{1,0:T(4,128)S(1)} %fusion.2.live_ref, bf16[8,512,128]{2,1,0:T(8,128)(2,1)S(1)} %copy-done, bf16[8,512,128]{2,1,0:T(8,128)(2,1)S(1)} %copy-done.1, ...), custom_call_target="tpu_custom_call" | custom-call | flops 2684354560 | bytes 2097152 | tf_op jit(solution)/shard_map/near_backward/near_backward/pallas_call | solution.py:287
  47.3 0.0 collective-permute-done.4
  47.3 1.3 %collective-permute-start.5 = (bf16[512,128]{1,0:T(8,128)(2,1)S(1)}, bf16[512,128]{1,0:T(8,128)(2,1)S(1)}, u32[]{:S(2)}, u32[]{:S(2)}) collective-permute-start(bf16[512,128]{1,0:T(8,128)(2,1)S(1)} %add_convert_fusion.3), channel_id=1, source_target_pairs={{4,0},{8,4},{12,8},{5,1},{9,5},{13,9},{6,2},{10,6},{14,10},{7,3},{... | collective-permute-start | bytes 393224 | tf_op jit(solution)/shard_map/back_k1/ppermute | solution.py:22
  48.6 0.0 collective-permute-done.6
  48.7 1.3 %collective-permute-start.7 = (bf16[512,128]{1,0:T(8,128)(2,1)S(1)}, bf16[512,128]{1,0:T(8,128)(2,1)S(1)}, u32[]{:S(2)}, u32[]{:S(2)}) collective-permute-start(bf16[512,128]{1,0:T(8,128)(2,1)S(1)} %add_convert_fusion.1), channel_id=1, source_target_pairs={{4,0},{8,4},{12,8},{5,1},{9,5},{13,9},{6,2},{10,6},{14,10},{7,3},{... | collective-permute-start | bytes 393224 | tf_op jit(solution)/shard_map/back_v1/ppermute | solution.py:22
  50.0 6.4 %collective-permute-done.5 = bf16[512,128]{1,0:T(8,128)(2,1)S(1)} collective-permute-done((bf16[512,128]{1,0:T(8,128)(2,1)S(1)}, bf16[512,128]{1,0:T(8,128)(2,1)S(1)}, u32[]{:S(2)}, u32[]{:S(2)}) %collective-permute-start.5) | collective-permute-done | bytes 131104 | tf_op jit(solution)/shard_map/back_k1/ppermute | solution.py:22
  56.3 0.7 %fusion = bf16[1,512,128]{2,1,0:T(8,128)(2,1)} fusion(f32[512,128]{1,0:T(8,128)S(1)} %get-tuple-element.22, bf16[512,128]{1,0:T(8,128)(2,1)S(1)} %collective-permute-done.5), kind=kLoop, calls=%fused_computation.5 | loop fusion | flops 196608 | bytes 524288 | tf_op jit(solution)/shard_map/broadcast_in_dim | solution.py:314
  57.0 0.8 %collective-permute-done.7 = bf16[512,128]{1,0:T(8,128)(2,1)S(1)} collective-permute-done((bf16[512,128]{1,0:T(8,128)(2,1)S(1)}, bf16[512,128]{1,0:T(8,128)(2,1)S(1)}, u32[]{:S(2)}, u32[]{:S(2)}) %collective-permute-start.7) | collective-permute-done | bytes 131104 | tf_op jit(solution)/shard_map/back_v1/ppermute | solution.py:22
  57.8 0.7 %fusion.1 = bf16[1,512,128]{2,1,0:T(8,128)(2,1)} fusion(f32[512,128]{1,0:T(8,128)S(1)} %get-tuple-element.25, bf16[512,128]{1,0:T(8,128)(2,1)S(1)} %collective-permute-done.7), kind=kLoop, calls=%fused_computation.6 | loop fusion | flops 196608 | bytes 524288 | tf_op jit(solution)/shard_map/broadcast_in_dim | solution.py:314
  (6 shorter events, 0.1 us)
Async XLA Ops:
  0.6 10.0 %collective-permute-start = (bf16[512,128]{1,0:T(8,128)(2,1)}, bf16[512,128]{1,0:T(8,128)(2,1)S(1)}, u32[]{:S(2)}, u32[]{:S(2)}) collective-permute-start(bf16[512,128]{1,0:T(8,128)(2,1)} %bitcast.17), channel_id=1, source_target_pairs={{0,4},{4,8},{8,12},{1,5},{5,9},{9,13},{2,6},{6,10},{10,14},{3,7},{... | collective-permute-start | bytes 393224 | tf_op jit(solution)/shard_map/hop_k1/ppermute | solution.py:22
  5.6 8.5 %collective-permute-start.2 = (bf16[512,128]{1,0:T(8,128)(2,1)}, bf16[512,128]{1,0:T(8,128)(2,1)S(1)}, u32[]{:S(2)}, u32[]{:S(2)}) collective-permute-start(bf16[512,128]{1,0:T(8,128)(2,1)} %bitcast.20), channel_id=1, source_target_pairs={{0,4},{4,8},{8,12},{1,5},{5,9},{9,13},{2,6},{6,10},{10,14},{3,7},{... | collective-permute-start | bytes 393224 | tf_op jit(solution)/shard_map/hop_v1/ppermute | solution.py:22
  10.6 17.5 %collective-permute-start.1 = (bf16[512,128]{1,0:T(8,128)(2,1)S(1)}, bf16[512,128]{1,0:T(8,128)(2,1)S(1)}, u32[]{:S(2)}, u32[]{:S(2)}) collective-permute-start(bf16[512,128]{1,0:T(8,128)(2,1)S(1)} %collective-permute-done.kp_ref), channel_id=1, source_target_pairs={{0,4},{4,8},{8,12},{1,5},{5,9},{9,13},{2,6},{6,10},{10,14},{3,7},{... | collective-permute-start | bytes 393224 | tf_op jit(solution)/shard_map/hop_k2/ppermute | solution.py:22
  14.1 14.1 %collective-permute-start.3 = (bf16[512,128]{1,0:T(8,128)(2,1)S(1)}, bf16[512,128]{1,0:T(8,128)(2,1)S(1)}, u32[]{:S(2)}, u32[]{:S(2)}) collective-permute-start(bf16[512,128]{1,0:T(8,128)(2,1)S(1)} %collective-permute-done.2.vp_ref), channel_id=1, source_target_pairs={{0,4},{4,8},{8,12},{1,5},{5,9},{9,13},{2,6},{6,10},{10,14},{3,7},{... | collective-permute-start | bytes 393224 | tf_op jit(solution)/shard_map/hop_v2/ppermute | solution.py:22
  17.2 1.2 %copy-start = (bf16[8,512,128]{2,1,0:T(8,128)(2,1)S(1)}, bf16[8,512,128]{2,1,0:T(8,128)(2,1)}, u32[]{:S(2)}) copy-start(bf16[8,512,128]{2,1,0:T(8,128)(2,1)} %q_ref.5) | copy-start | bytes 3145732
  18.5 0.9 %copy-start.2 = (bf16[1,512,128]{2,1,0:T(8,128)(2,1)S(1)}, bf16[1,512,128]{2,1,0:T(8,128)(2,1)}, u32[]{:S(2)}) copy-start(bf16[1,512,128]{2,1,0:T(8,128)(2,1)} %param.8) | copy-start | bytes 393220
  19.4 0.9 %copy-start.3 = (bf16[1,512,128]{2,1,0:T(8,128)(2,1)S(1)}, bf16[1,512,128]{2,1,0:T(8,128)(2,1)}, u32[]{:S(2)}) copy-start(bf16[1,512,128]{2,1,0:T(8,128)(2,1)} %param.9) | copy-start | bytes 393220
  20.3 7.9 %copy-start.1 = (bf16[8,512,128]{2,1,0:T(8,128)(2,1)S(1)}, bf16[8,512,128]{2,1,0:T(8,128)(2,1)}, u32[]{:S(2)}) copy-start(bf16[8,512,128]{2,1,0:T(8,128)(2,1)} %do_ref.3) | copy-start | bytes 3145732
  35.9 11.4 %collective-permute-start.4 = (bf16[512,128]{1,0:T(8,128)(2,1)S(1)}, bf16[512,128]{1,0:T(8,128)(2,1)S(1)}, u32[]{:S(2)}, u32[]{:S(2)}) collective-permute-start(bf16[512,128]{1,0:T(8,128)(2,1)S(1)} %bitcast.24), channel_id=1, source_target_pairs={{4,0},{8,4},{12,8},{5,1},{9,5},{13,9},{6,2},{10,6},{14,10},{7,3},{... | collective-permute-start | bytes 393224 | tf_op jit(solution)/shard_map/back_k2/ppermute | solution.py:22
  37.1 11.5 %collective-permute-start.6 = (bf16[512,128]{1,0:T(8,128)(2,1)S(1)}, bf16[512,128]{1,0:T(8,128)(2,1)S(1)}, u32[]{:S(2)}, u32[]{:S(2)}) collective-permute-start(bf16[512,128]{1,0:T(8,128)(2,1)S(1)} %bitcast.23), channel_id=1, source_target_pairs={{4,0},{8,4},{12,8},{5,1},{9,5},{13,9},{6,2},{10,6},{14,10},{7,3},{... | collective-permute-start | bytes 393224 | tf_op jit(solution)/shard_map/back_v2/ppermute | solution.py:22
  47.3 9.0 %collective-permute-start.5 = (bf16[512,128]{1,0:T(8,128)(2,1)S(1)}, bf16[512,128]{1,0:T(8,128)(2,1)S(1)}, u32[]{:S(2)}, u32[]{:S(2)}) collective-permute-start(bf16[512,128]{1,0:T(8,128)(2,1)S(1)} %add_convert_fusion.3), channel_id=1, source_target_pairs={{4,0},{8,4},{12,8},{5,1},{9,5},{13,9},{6,2},{10,6},{14,10},{7,3},{... | collective-permute-start | bytes 393224 | tf_op jit(solution)/shard_map/back_k1/ppermute | solution.py:22
  48.7 9.1 %collective-permute-start.7 = (bf16[512,128]{1,0:T(8,128)(2,1)S(1)}, bf16[512,128]{1,0:T(8,128)(2,1)S(1)}, u32[]{:S(2)}, u32[]{:S(2)}) collective-permute-start(bf16[512,128]{1,0:T(8,128)(2,1)S(1)} %add_convert_fusion.1), channel_id=1, source_target_pairs={{4,0},{8,4},{12,8},{5,1},{9,5},{13,9},{6,2},{10,6},{14,10},{7,3},{... | collective-permute-start | bytes 393224 | tf_op jit(solution)/shard_map/back_v1/ppermute | solution.py:22
